TPU v7x, 128 devices: a whole 4x4x4 slice. The times are simulated.
128 devices in a mesh: gx: 16 (over z_lo, x, core), gz: 8 (over y, z_hi).
Axes of the slice: x: 4, y: 4, z: 4 (z_hi: 2, z_lo: 2; z = z_hi * 2 + z_lo), core: 2. Of those that a mesh axis runs over, the one named last changes fastest.
Arguments:
- elevation: float32 [2048, 2048], P(('gx', 'gz')), may hold values from -2 to 2
- potential: float32 [2048, 2048], P(('gx', 'gz')), may hold values from -6 to 6
- tracer: float32 [2048, 64, 256], P('gx', 'gz'), may hold values from -6 to 6
- wind_speed: float32 [2048, 64, 256], P('gx', 'gz'), may hold values from -4 to 4
Outputs:
- new_elevation: float32 [2048, 2048], P(('gx', 'gz'))
- new_tracer: float32 [2048, 64, 256], P('gx', 'gz')
All inputs are finite; a program needn't handle non-finite values.
Results may differ from a plain program's by a relative error of at most 0.00019.
Values sent between devices are 32-bit elements; how exact they have to be, the bound alone decides.
No kernel may reach another device: no remote copies, remote signals or barrier semaphores. Data moves between devices by JAX's collectives and lax.ppermute only.
A program may use at most 128 MiB of HBM per device.

v0:
```python
import functools

import jax
import jax.numpy as jnp
import ml_dtypes
import numpy as np
from jax import lax
from jax.experimental import pallas as pl
from jax.experimental.pallas import tpu as pltpu
from jax.sharding import PartitionSpec as P

NS = 2048
DT_WAVE = 0.05
COLUMN_DEPTH = 32.0
DT_AIR = 0.1
NU_AIR = 0.2
TWO_PI = 6.283185307179586
WAVE_UNIT = TWO_PI / NS
BOTH = ("gx", "gz")
F32 = jnp.float32
BF16 = jnp.bfloat16


def halves(matrix):
    exact = np.asarray(matrix, np.float64)
    lead = exact.astype(np.float32).astype(ml_dtypes.bfloat16)
    rest = (exact - lead.astype(np.float64)).astype(np.float32).astype(ml_dtypes.bfloat16)
    return np.stack([lead, rest])


@functools.cache
def tables():
    n128, n16 = np.arange(128), np.arange(16)
    eye16, eye8 = np.eye(16), np.eye(8)
    turn = 2 * np.pi * (np.outer(n128, n128) % 128) / 128
    c, s = np.cos(turn), np.sin(turn)
    wheel = np.concatenate([c, s], 0)
    edge = np.zeros((2, 128, 2, 128))
    edge_back = np.zeros((2, 128, 2, 128))
    sign = (-1.0) ** n128
    for d in range(128):
        if d < 64:
            angle, part = 2 * np.pi * n128 * d / 128, 0
        else:
            angle, part = 2 * np.pi * n128 * (2 * (d - 64) + 1) / 256, 1
        edge[0, d, part] = np.cos(angle)
        edge[1, d, part] = -np.sin(angle) if d else sign
        weight = 2.0 if d else 1.0
        edge_back[part, :, 0, d] = weight * np.cos(angle)
        edge_back[part, :, 1, d] = -weight * np.sin(angle) if d else sign
    edge = edge.reshape(256, 256)
    edge_back = edge_back.reshape(256, 256)
    k8 = np.arange(8)
    angle = 2 * np.pi * np.outer(n16, k8) / 16
    near_re, near_im = np.cos(angle), -np.sin(angle)
    near_im[:, 0] = (-1.0) ** n16
    weight = np.where(k8 == 0, 1.0, 2.0)
    near = np.zeros((16, 16, 2, 8, 16))
    near_back = np.zeros((2, 8, 16, 16, 16))
    for part, table in enumerate((near_re, near_im)):
        near[:, :, part] = table[:, None, :, None] * eye16[None, :, None, :]
        near_back[part] = (table * weight).T[:, None, :, None] * eye16[None, :, None, :]
    near = near.reshape(256, 256)
    near_back = near_back.reshape(256, 256)
    angle = 2 * np.pi * np.outer(n16, n16) / 16
    cx, sx = np.kron(eye8, np.cos(angle)), np.kron(eye8, np.sin(angle))
    comb = np.concatenate([cx, sx], 0)
    y_angle = 2 * np.pi * np.repeat(np.outer(n128, k8), 16, axis=1) / NS
    x_angle = 2 * np.pi * np.tile(np.outer(n128, n16), (1, 8)) / NS
    twist = lambda a: np.stack([np.cos(a), -np.sin(a)]).astype(np.float32)
    r = n128[None, :, None, None]
    x = 16 * n128[None, None, :, None] + n16.reshape(4, 1, 1, 4)
    n = r - x
    with np.errstate(divide="ignore", invalid="ignore"):
        slope = np.where(n % NS == 0, 0.0, (np.pi / NS) * (-1.0) ** (n % 2) / np.tan(np.pi * n / NS))
    slope = slope.reshape(512, 512)
    return dict(
        wheel=halves(wheel),
        edge=halves(edge),
        edge_back=halves(edge_back),
        near=halves(near),
        near_back=halves(near_back),
        comb=halves(comb),
        twist_y=twist(y_angle),
        twist_x=twist(x_angle),
        slope=halves(slope),
    )


def dot(a, b):
    return jnp.dot(a, b, preferred_element_type=F32)


def split(x):
    lead = x.astype(BF16)
    return lead, (x - lead.astype(F32)).astype(BF16)


def from_left(table, x):
    lead, rest = split(x)
    width = x.shape[1]
    both = dot(table[0], jnp.concatenate([lead, rest], 1))
    return both[:, :width] + both[:, width:] + dot(table[1], lead)


def from_right(x, table):
    lead, rest = split(x)
    rows = x.shape[0]
    both = dot(jnp.concatenate([lead, rest], 0), table[0])
    return both[:rows] + both[rows:] + dot(lead, table[1])


def turning(table, sign):
    blocks = []
    for half in (table[0], table[1]):
        c, s = half[:128], half[128:]
        upper, lower = (s, -s) if sign > 0 else (-s, s)
        rows = [jnp.concatenate([c, upper], 1), jnp.concatenate([lower, c], 1)]
        blocks.append(jnp.concatenate(rows, 0))
    return blocks


def slot_zero(shape):
    return lax.broadcasted_iota(jnp.int32, shape, 1) % 128 < 16


def y_twisted(t, parts):
    re, im = parts[:, :128], parts[:, 128:]
    c, s = t["twist_y"][0], t["twist_y"][1]
    return jnp.concatenate([re * c - im * s, re * s + im * c], 0)


def y_joined(t, parts, usual):
    first = from_left(t["edge"], parts)
    out = jnp.where(slot_zero(usual.shape), first, usual)
    return out[:128], out[128:]


def y_forward(t, field):
    parts = y_twisted(t, from_right(field, t["near"]))
    return y_joined(t, parts, from_left(turning(t["wheel"], 1), parts))


def y_back_far(t, re, im):
    parts = jnp.concatenate([re, im], 0)
    usual = from_left(turning(t["wheel"], -1), parts)
    first = from_left(t["edge_back"], parts)
    parts = jnp.where(slot_zero(usual.shape), first, usual)
    c, s = t["twist_y"][0], t["twist_y"][1]
    out = []
    for at in range(0, parts.shape[1], 128):
        re, im = parts[:128, at : at + 128], parts[128:, at : at + 128]
        out.append(jnp.concatenate([re * c + im * s, im * c - re * s], 1))
    return out


def y_back(t, re, im):
    return from_right(y_back_far(t, re, im)[0], t["near_back"])


def x_forward(t, re, im, mirrored):
    parts = jnp.concatenate([re, im], 0)
    if mirrored:
        parts = jnp.concatenate([parts, jnp.concatenate([re, -im], 0)], 1)
    parts = from_left(turning(t["wheel"], 1), parts)
    c, s = t["twist_x"][0], t["twist_x"][1]
    rows = []
    for at in range(0, parts.shape[1], 128):
        re, im = parts[:128, at : at + 128], parts[128:, at : at + 128]
        rows.append(jnp.concatenate([re * c - im * s, re * s + im * c], 1))
    parts = from_right(jnp.concatenate(rows, 0) if mirrored else rows[0], turning(t["comb"], -1))
    out = parts[:128, :128], parts[:128, 128:]
    if mirrored:
        out += parts[128:, :128], parts[128:, 128:]
    return out


def x_back(t, re, im):
    parts = from_right(jnp.concatenate([re, im], 1), turning(t["comb"], 1))
    re, im = parts[:, :128], parts[:, 128:]
    c, s = t["twist_x"][0], t["twist_x"][1]
    parts = jnp.concatenate([re * c + im * s, im * c - re * s], 0)
    out = from_left(turning(t["wheel"], -1), parts)
    return out[:128], out[128:]


def x_waves():
    q1 = lax.broadcasted_iota(jnp.int32, (128, 128), 0)
    lane = lax.broadcasted_iota(jnp.int32, (128, 128), 1)
    kx = q1 + 128 * (lane % 16)
    return jnp.where(kx < NS // 2, kx, kx - NS)


def odd_x():
    kx = x_waves()
    return jnp.where(kx == -(NS // 2), 0, kx).astype(F32) * WAVE_UNIT


def squared_waves(device):
    slot = lax.broadcasted_iota(jnp.int32, (128, 128), 1) // 16
    first = jnp.where(device < 64, 16 * device, 8 + 16 * (device - 64))
    ky = jnp.where(slot == 0, first, slot + 16 * device)
    other = jnp.where((slot == 0) & (device == 0), NS // 2, ky)
    fold = lambda k: jnp.where(k > NS // 2, NS - k, k).astype(F32) * WAVE_UNIT
    wave_x = x_waves().astype(F32) * WAVE_UNIT
    return wave_x * wave_x + fold(ky) * fold(ky), wave_x * wave_x + fold(other) * fold(other)


def even_filter(spectrum, on_re, on_im):
    re, im, mirror_re, mirror_im = spectrum
    plus = (on_re + on_im) * (0.5 / (NS * NS))
    minus = (on_re - on_im) * (0.5 / (NS * NS))
    return re * plus + mirror_re * minus, im * plus + mirror_im * minus


def power_filter(spectrum, squares, power):
    factors = []
    for square in squares:
        magnitude = jnp.sqrt(square)
        factors.append({1: magnitude, 2: square, 3: square * magnitude}[power])
    return even_filter(spectrum, *factors)


def x_derivative(re, im, scale):
    factor = odd_x() * scale
    return -factor * im, factor * re


def y_derivative(re, im):
    d = lax.broadcasted_iota(jnp.int32, (128, 128), 0)
    slot = lax.broadcasted_iota(jnp.int32, (128, 128), 1) // 16
    first = jnp.where(d < 64, 16 * d, 8 + 16 * (d - 64))
    ky = jnp.where(slot == 0, first, slot + 16 * d)
    factor = jnp.where(ky < NS // 2, ky, ky - NS).astype(F32) * (WAVE_UNIT / NS)
    return -factor * im, factor * re


def to_lanes(rows):
    return jnp.concatenate([rows[:, 128 * a : 128 * a + 128] for a in range(16)], 0).T


def pick(ref, fields, index):
    step = 2 * fields
    return ref[pl.ds(2 * index, 128, step), :], ref[pl.ds(2 * index + 1, 128, step), :]


def put(ref, fields, index, values):
    step = 2 * fields
    ref[pl.ds(2 * index, 128, step), :] = values[0]
    ref[pl.ds(2 * index + 1, 128, step), :] = values[1]


def near_core(array):
    return pltpu.with_memory_space_constraint(array, pltpu.VMEM)


def far_away(array):
    return pltpu.with_memory_space_constraint(array, pltpu.HBM)


def run(body, names, outs, *arrays, held, scalars=None, scratch=(), far=()):
    consts = [near_core(held[name]) for name in names]
    lead = [] if scalars is None else [scalars]
    arrays = [far_away(a) if i in far else near_core(a) for i, a in enumerate(arrays)]

    def kernel(*refs):
        at = len(lead)
        tabs = dict(zip(names, refs[at : at + len(names)]))
        body(tabs, *refs[:at], *refs[at + len(names) :])

    vmem = pl.BlockSpec(memory_space=pltpu.VMEM)
    smem = pl.BlockSpec(memory_space=pltpu.SMEM)
    place = lambda out: (pltpu.VMEM if out[-1] == "near" else pltpu.HBM)(out[:2], F32)
    return pl.pallas_call(
        kernel,
        out_shape=[place(out) for out in outs],
        in_specs=[smem] * len(lead) + [vmem] * (len(consts) + len(arrays)),
        out_specs=[vmem] * len(outs),
        scratch_shapes=list(scratch),
        compiler_params=pltpu.CompilerParams(vmem_limit_bytes=16 << 20),
    )(*lead, *consts, *arrays)


Y_FWD = ("near", "wheel", "edge", "twist_y")
Y_BACK = ("near_back", "wheel", "edge_back", "twist_y")
Y_BOTH = ("near", "wheel", "edge", "twist_y", "near_back", "edge_back")
X_BOTH = ("wheel", "comb", "twist_x")
PLANES = (256, 128)
FIELD = (128, 256, "near")
NAMES = ("wheel", "comb", "twist_x", "near", "near_back", "edge", "edge_back", "twist_y")


def start_rows(potential):
    names = ("near", "twist_y", "wheel", "edge")
    sources = [potential] + [jnp.asarray(tables()[name]) for name in names]
    count = len(sources)

    def rows_start(*refs):
        inputs, send, held, sems = refs[:count], refs[count], refs[count + 1 : -1], refs[-1]
        copies = [pltpu.make_async_copy(inputs[i], held[i], sems.at[i]) for i in range(count)]
        for copy in copies:
            copy.start()
        t = dict(zip(names, held[1:]))
        copies[0].wait()
        field = to_lanes(held[0][...])
        copies[1].wait()
        parts = from_right(field, t["near"])
        copies[2].wait()
        parts = y_twisted(t, parts)
        copies[3].wait()
        usual = from_left(turning(t["wheel"], 1), parts)
        copies[4].wait()
        put(send, 1, 0, y_joined(t, parts, usual))

    return pl.pallas_call(
        rows_start,
        out_shape=pltpu.HBM(PLANES, F32),
        in_specs=[pl.BlockSpec(memory_space=pltpu.HBM)] * count,
        out_specs=pl.BlockSpec(memory_space=pltpu.VMEM),
        scratch_shapes=[pltpu.VMEM(c.shape, c.dtype) for c in sources]
        + [pltpu.SemaphoreType.DMA((count,))],
        compiler_params=pltpu.CompilerParams(vmem_limit_bytes=16 << 20),
        name="rows_start",
    )(*[far_away(source) for source in sources])


def hold_tables():
    consts = [jnp.asarray(tables()[name]) for name in NAMES]
    count = len(consts)

    def hold(*refs):
        sems = refs[-1]
        copies = [
            pltpu.make_async_copy(refs[i], refs[count + i], sems.at[i]) for i in range(count)
        ]
        for copy in copies:
            copy.start()
        for copy in copies:
            copy.wait()

    out = pl.pallas_call(
        hold,
        out_shape=[pltpu.VMEM(c.shape, c.dtype) for c in consts],
        in_specs=[pl.BlockSpec(memory_space=pltpu.HBM)] * count,
        out_specs=[pl.BlockSpec(memory_space=pltpu.VMEM)] * count,
        scratch_shapes=[pltpu.SemaphoreType.DMA((count,))],
        compiler_params=pltpu.CompilerParams(vmem_limit_bytes=16 << 20),
        name="hold_tables",
    )(*[far_away(c) for c in consts])
    return dict(zip(NAMES, out))


def stacked(ref):
    return [ref[128 * i : 128 * i + 128, :] for i in range(ref.shape[0] // 128)]


def rows_surface(t, eta, send, lanes, again, window):
    lanes[...] = to_lanes(eta[...])
    window[0:16, :], window[16:32, :] = eta[:, 0:128], eta[:, 128:256]
    spectrum = y_forward(t, lanes[...])
    put(send, 1, 0, spectrum)
    again[0:128, :], again[128:256, :] = spectrum


def rows_along(t, start, surface, along):
    slope = y_back(t, *y_derivative(surface[0:128, :], surface[128:256, :]))
    along[0:128, :] = 1.0 + slope * slope
    along[128:256, :] = slope * y_back(t, *y_derivative(*pick(start, 1, 0)))


def columns_first(t, device, got, send, held):
    spectrum = x_forward(t, *pick(got, 1, 0), True)
    for i, part in enumerate(spectrum):
        held[128 * i : 128 * i + 128, :] = part
    put(send, 1, 0, x_back(t, *power_filter(spectrum, squared_waves(device[0]), 1)))


def columns_first_late(t, device, held, late):
    spectrum = stacked(held)
    squares = squared_waves(device[0])
    put(late, 3, 0, x_back(t, *power_filter(spectrum, squares, 2)))
    put(late, 3, 1, x_back(t, *power_filter(spectrum, squares, 3)))
    put(late, 3, 2, x_back(t, *x_derivative(spectrum[0], spectrum[1], 1.0 / (NS * NS))))


def rows_second(t, got, lanes, surface, send, once):
    once[...] = y_back(t, *pick(got, 1, 0))
    put(send, 2, 0, y_forward(t, -lanes[...] * once[...]))
    put(send, 2, 1, pick(surface, 1, 0))


def columns_second(t, device, got, late, send, held):
    spectrum = x_forward(t, *pick(got, 2, 0), True)
    for i, part in enumerate(spectrum):
        held[128 * i : 128 * i + 128, :] = part
    for i, part in enumerate(pick(got, 2, 1)):
        held[512 + 128 * i : 640 + 128 * i, :] = part
    put(send, 4, 0, x_back(t, *power_filter(spectrum, squared_waves(device[0]), 1)))
    for index in range(3):
        put(send, 4, 1 + index, pick(late, 3, index))


def columns_second_late(t, device, held, late):
    parts = stacked(held)
    put(late, 2, 0, x_back(t, *power_filter(parts[:4], squared_waves(device[0]), 2)))
    re, im = x_forward(t, parts[4], parts[5], False)
    put(late, 2, 1, x_back(t, *x_derivative(re, im, 1.0 / (NS * NS))))


def rows_third(t, got, lanes, send, once, twice):
    eta = lanes[...]
    once[...] = y_back(t, *pick(got, 4, 0))
    twice[...] = y_back(t, *pick(got, 4, 1))
    third = -eta * once[...] - 0.5 * eta * eta * twice[...]
    put(send, 1, 0, y_forward(t, third))


def rows_third_late(t, got, lanes, first_once, once, twice, ready):
    eta = lanes[...]
    thrice = y_back(t, *pick(got, 4, 2))
    ready[0:128, :] = y_back(t, *pick(got, 4, 3))
    ready[128:256, :] = first_once[...] + eta * twice[...] + 0.5 * eta * eta * thrice + once[...]


def columns_third(t, device, got, late, send):
    spectrum = x_forward(t, *pick(got, 1, 0), True)
    put(send, 3, 0, x_back(t, *power_filter(spectrum, squared_waves(device[0]), 1)))
    for index in range(2):
        put(send, 3, 1 + index, pick(late, 2, index))


def rows_finish(t, got, lanes, ready, along, new_rows, send, window):
    pairs = [pick(got, 3, i) for i in range(3)]
    parts = y_back_far(t, *[jnp.concatenate(pair, 1) for pair in zip(*pairs)])
    back = from_right(jnp.concatenate(parts, 0), t["near_back"])
    third_once, second_twice, slope_x = back[:128], back[128:256], back[256:]
    eta = lanes[...]
    speed, known, factor, cross = [ref[at : at + 128, :] for ref in (ready, along) for at in (0, 128)]
    tendency = -(slope_x * speed + cross) + (factor + slope_x * slope_x) * (
        known + third_once + eta * second_twice
    )
    new = (eta + DT_WAVE * tendency).T
    window[...] = new[:32]
    for a in range(16):
        new_rows[:, 128 * a : 128 * a + 128] = new[16 * a : 16 * a + 16]
    group = lax.broadcasted_iota(jnp.int32, (16, 128), 1) // 32
    blocks = []
    for a in range(2):
        rows = new[16 * a : 16 * a + 16]
        turned = [rows] + [pltpu.roll(rows, 32 * k, 1) for k in range(1, 4)]
        for chunk in range(4):
            block = jnp.zeros((4, 128), F32)
            for g in range(4):
                moved = turned[(g - chunk) % 4]
                block = block + jnp.where(group == g, moved, 0.0)[4 * g : 4 * g + 4]
            blocks.append(block)
    block = jnp.concatenate(blocks, 0)
    for at in range(16):
        send[32 * at : 32 * at + 32, :] = block


def columns_slope(t, slab, got, window, table, send, twofold):
    twofold[0:512, :] = got[...]
    twofold[512:1024, :] = got[...]
    start = pl.multiple_of(slab[0] * 32, 32)
    full = from_left(table, twofold[pl.ds(start, 512), :])
    group = lax.broadcasted_iota(jnp.int32, (128, 128), 1) // 32
    total = jnp.zeros((128, 128), F32)
    for g in range(4):
        total = total + jnp.where(group == g, full[128 * g : 128 * g + 128], 0.0)
    total = total + pltpu.roll(total, 64, 1)
    total = total + pltpu.roll(total, 32, 1)
    slope = total.T[:32]
    for at in range(8):
        send[64 * at : 64 * at + 32, :] = slope
        send[64 * at + 32 : 64 * at + 64, :] = window[...]


LEVELS = 8


def block_rows(block, half, level):
    return pl.ds(pl.multiple_of(128 * block + 64 * half + 8 * level, 8), 8)


def rim_rows(block, half, level):
    return pl.ds(pl.multiple_of(256 * half + 128 * level + 8 * block, 8), 8)


def exchanged(v):
    row = lax.broadcasted_iota(jnp.int32, (8, 128), 0)
    for step in (4, 2, 1):
        keep = (row & step) == 0
        out = list(v)
        for i in range(8):
            if not i & step:
                a, b = v[i], v[i + step]
                out[i] = jnp.where(keep, a, pltpu.roll(b, step, 0))
                out[i + step] = jnp.where(keep, pltpu.roll(a, 8 - step, 0), b)
        v = out
    return v


def air_moved(
    place, tracer, wind, before, after, moved, drift, bottom, top, q_s, w_s, moved_s, drift_s, sems
):
    pitch = 2 * LEVELS
    rows = [pl.ds(512 * part, 512) for part in range(4)]
    copies = [
        (before, q_s.at[pl.ds(0, pitch)]),
        (after, q_s.at[pl.ds(pitch + 2048, pitch)]),
    ]
    for part in range(4):
        copies.append((tracer.at[rows[part]], q_s.at[pl.ds(pitch + 512 * part, 512)]))
        copies.append((wind.at[rows[part]], w_s.at[rows[part]]))
    copies = [pltpu.make_async_copy(*pair, sems.at[i]) for i, pair in enumerate(copies)]
    for copy in copies:
        copy.start()
    for copy in copies[:4]:
        copy.wait()
    lane = lax.broadcasted_iota(jnp.int32, (8, 128), 1)
    first, last = lane == 0, lane == 127
    total = (LEVELS * place[1]).astype(F32)
    lifts = [1.0 - ((place[0] * LEVELS + level).astype(F32) + 0.5) / total for level in range(LEVELS)]
    scales = [lift * (DT_AIR * 0.5 * total) for lift in lifts]

    def step(block, carry):
        moved_x, wind_x = ([], []), ([], [])
        for x in range(8):
            at = pl.multiple_of((block * 8 + x) * pitch, pitch)

            def both(ref, shift):
                return [ref[pl.ds(at + shift * pitch + 8 * half, 8), :] for half in range(2)]

            west, mid, east, w = both(q_s, 0), both(q_s, 1), both(q_s, 2), both(w_s, 0)
            back = [pltpu.roll(q, 127, 1) for q in mid]
            ahead = [pltpu.roll(q, 1, 1) for q in mid]
            north = [jnp.where(last, back[1], back[0]), jnp.where(last, mid[1], back[1])]
            south = [jnp.where(first, mid[0], ahead[0]), jnp.where(first, ahead[0], ahead[1])]
            for half in range(2):
                moved_x[half].append(
                    mid[half]
                    + DT_AIR
                    * (
                        -w[half] * (east[half] - west[half]) * 0.5
                        + NU_AIR
                        * (east[half] + west[half] + north[half] + south[half] - 4.0 * mid[half])
                    )
                )
                wind_x[half].append(w[half])
        for half in range(2):
            by_level = exchanged(moved_x[half])
            for level, q in enumerate(by_level):
                moved_s[block_rows(block, half, level), :] = q
            for k in range(2):
                bottom[rim_rows(block, half, k), :] = by_level[k]
                top[rim_rows(block, half, k), :] = by_level[LEVELS - 2 + k]
            for level, w in enumerate(exchanged(wind_x[half])):
                drift_s[block_rows(block, half, level), :] = w * scales[level]
        return carry

    results = []
    for part in range(4):
        for copy in copies[4 + 2 * part : 6 + 2 * part]:
            copy.wait()
        lax.fori_loop(4 * part, 4 * part + 4, step, 0)
        for i, (source, target) in enumerate(((moved_s, moved), (drift_s, drift))):
            out = pltpu.make_async_copy(
                source.at[rows[part]], target.at[rows[part]], sems.at[10 + 2 * part + i]
            )
            out.start()
            results.append(out)
    for out in results:
        out.wait()


def air_finish(place, got, before, moved, drift, below, above, out, *scratch):
    ratio_s, inverse_s, spread_s, slope_s, out_s, sems = scratch
    group, groups = place[0], place[1]
    total = (LEVELS * groups).astype(F32)
    lowest, highest = group == 0, group == groups - 1

    def lift_of(level):
        return 1.0 - ((group * LEVELS + level).astype(F32) + 0.5) / total

    def remap(lower, mid, upper, shift):
        return mid + (0.5 * shift) * ((upper - lower) + shift * (upper - 2.0 * mid + lower))

    slope_s[...] = jnp.concatenate([got[64 * g : 64 * g + 32, :] for g in range(8)], 0).T
    for g in range(8):
        for a in range(2):
            at = 64 * g + 32 + 16 * a
            from_old = pl.multiple_of(jnp.bitwise_xor(group, g) * 32 + 16 * a, 16)
            rows, lanes = slice(16 * g, 16 * g + 16), slice(128 * a, 128 * a + 128)
            new, old = got[at : at + 16, :], before[pl.ds(from_old, 16), :]
            ratio_s[rows, lanes] = (new - old) / (COLUMN_DEPTH - old) * total
            inverse = 1.0 / (COLUMN_DEPTH - new)
            inverse_s[rows, lanes] = inverse * slope_s[rows, lanes]
            spread_s[rows, lanes] = inverse * inverse * (DT_AIR * NU_AIR * total * total)
    lifts = [lift_of(jnp.int32(level)) for level in range(-1, LEVELS + 1)]

    def step(block, carry):
        rows = pl.ds(pl.multiple_of(8 * block, 8), 8)
        for half in range(2):
            lanes = slice(128 * half, 128 * half + 128)
            m = [moved[block_rows(block, half, level), :] for level in range(LEVELS)]
            low = jnp.where(lowest, m[0], below[rim_rows(block, half, 1), :])
            high = jnp.where(highest, m[-1], above[rim_rows(block, half, 0), :])
            outer = [ref[rim_rows(block, half, k), :] for ref, k in ((below, 0), (above, 1))]
            m = [outer[0], low] + m + [high, outer[1]]
            ratio = ratio_s[rows, lanes]
            r = [
                remap(m[i], m[i + 1], m[i + 2], ratio * lifts[i]) for i in range(LEVELS + 2)
            ]
            r[0] = jnp.where(lowest, r[1], r[0])
            r[-1] = jnp.where(highest, r[-2], r[-1])
            inverse, spread = inverse_s[rows, lanes], spread_s[rows, lanes]
            results = []
            for level in range(LEVELS):
                lower, mid, upper = r[level], r[level + 1], r[level + 2]
                results.append(
                    mid
                    + spread * (upper - 2.0 * mid + lower)
                    + drift[block_rows(block, half, level), :] * inverse * (upper - lower)
                )
            for x, value in enumerate(exchanged(results)):
                at = pl.multiple_of((block * 8 + x) * 16 + 8 * half, 8)
                out_s[pl.ds(at, 8), :] = value
        return carry

    copies = []
    for quarter in range(4):
        lax.fori_loop(4 * quarter, 4 * quarter + 4, step, 0)
        rows = pl.ds(512 * quarter, 512)
        copies.append(pltpu.make_async_copy(out_s.at[rows], out.at[rows], sems.at[quarter]))
        copies[-1].start()
    for copy in copies:
        copy.wait()


def air_moved_call(place, tracer, wind, before, after):
    hbm = pl.BlockSpec(memory_space=pltpu.HBM)
    vmem = pl.BlockSpec(memory_space=pltpu.VMEM)
    return pl.pallas_call(
        air_moved,
        out_shape=[pltpu.HBM((2048, 128), F32)] * 2 + [pltpu.HBM((512, 128), F32)] * 2,
        in_specs=[pl.BlockSpec(memory_space=pltpu.SMEM)] + [hbm] * 4,
        out_specs=[hbm, hbm, vmem, vmem],
        scratch_shapes=[
            pltpu.VMEM((2080, 128), F32),
            pltpu.VMEM((2048, 128), F32),
            pltpu.VMEM((2048, 128), F32),
            pltpu.VMEM((2048, 128), F32),
            pltpu.SemaphoreType.DMA((18,)),
        ],
        compiler_params=pltpu.CompilerParams(vmem_limit_bytes=24 << 20),
        name="air_moved",
    )(place, *[far_away(a) for a in (tracer, wind, before, after)])


def air_finish_call(place, got, old, moved, drift, below, above):
    vmem = pl.BlockSpec(memory_space=pltpu.VMEM)
    near = [near_core(a) for a in (got, old, moved, drift, below, above)]
    return pl.pallas_call(
        air_finish,
        out_shape=pltpu.HBM((2048, 128), F32),
        in_specs=[pl.BlockSpec(memory_space=pltpu.SMEM)] + [vmem] * 6,
        out_specs=pl.BlockSpec(memory_space=pltpu.HBM),
        scratch_shapes=[pltpu.VMEM((128, 256), F32)] * 4
        + [pltpu.VMEM((2048, 128), F32), pltpu.SemaphoreType.DMA((4,))],
        compiler_params=pltpu.CompilerParams(vmem_limit_bytes=16 << 20),
        name="air_finish",
    )(place, *near)


def split_halves(air):
    return air.reshape(128, LEVELS, 2, 128).transpose(0, 2, 1, 3).reshape(2048, 128)


def exchange(buffer, axes=BOTH, fields=1):
    if fields == 3:
        buffer = buffer.reshape(128, 3, 2, 128)
    out = lax.all_to_all(buffer, axes, split_axis=0, concat_axis=0, tiled=True)
    return out.reshape(-1, 128)


def shards(elevation, potential, tracer, wind_speed):
    gx, gz = lax.axis_index("gx"), lax.axis_index("gz")
    groups = lax.axis_size("gz")
    device = (gx * groups + gz).astype(jnp.int32).reshape(1)
    slab = gx.astype(jnp.int32).reshape(1)
    place = jnp.concatenate([gz.astype(jnp.int32).reshape(1), jnp.full((1,), groups, jnp.int32)])
    quantity, wind = split_halves(tracer), split_halves(wind_speed)
    size = lax.axis_size("gx")
    ring = [(i, (i + 1) % size) for i in range(size)]
    rise = [(i, i + 1) for i in range(groups - 1)]
    back = lambda pairs: [(j, i) for i, j in pairs]

    start = start_rows(potential)
    got = exchange(start)
    t = hold_tables()
    surface, lanes, spectrum, old = run(
        rows_surface,
        Y_FWD,
        [(256, 128, "near"), FIELD, PLANES, (32, 128)],
        elevation,
        held=t,
        far=(0,),
    )

    send, held = run(
        columns_first, X_BOTH, [(256, 128, "near"), (512, 128, "near")], got, scalars=device, held=t
    )
    got = exchange(send)
    (late,) = run(columns_first_late, X_BOTH, [(768, 128, "near")], held, scalars=device, held=t)
    before = lax.ppermute(quantity[-16:], "gx", ring)
    after = lax.ppermute(quantity[:16], "gx", back(ring))

    for step in range(3):
        pairs = [(i, i ^ (1 << step)) for i in range(groups)]
        old = jnp.concatenate([old, lax.ppermute(old, "gz", pairs)], 0)

    send, first_once = run(rows_second, Y_BOTH, [(512, 128), FIELD], got, lanes, surface, held=t)
    got = exchange(send)
    moved, drift, bottom, top = air_moved_call(place, quantity, wind, before, after)

    send, held = run(
        columns_second,
        X_BOTH,
        [(1024, 128), (768, 128, "near")],
        got,
        late,
        scalars=device,
        held=t,
    )
    got = exchange(send)
    (late,) = run(columns_second_late, X_BOTH, [(512, 128, "near")], held, scalars=device, held=t)
    below = lax.ppermute(top, "gz", rise)
    above = lax.ppermute(bottom, "gz", back(rise))

    send, once, twice = run(rows_third, Y_BOTH, [PLANES, FIELD, FIELD], got, lanes, held=t)
    got_rows, got = got, exchange(send)
    (ready,) = run(
        rows_third_late,
        Y_BACK,
        [(256, 256, "near")],
        got_rows,
        lanes,
        first_once,
        once,
        twice,
        held=t,
    )

    (along,) = run(rows_along, Y_BACK, [(256, 256, "near")], start, spectrum, held=t, far=(0, 1))

    (send,) = run(columns_third, X_BOTH, [(768, 128)], got, late, scalars=device, held=t)
    got = exchange(send, fields=3)

    new_rows, send, window = run(
        rows_finish,
        Y_BACK,
        [(16, NS, "near"), (512, 128, "near"), (32, 128, "near")],
        got,
        lanes,
        ready,
        along,
        held=t,
    )
    got = exchange(send)
    (send,) = run(
        columns_slope,
        (),
        [(512, 128, "near")],
        got,
        window,
        jnp.asarray(tables()["slope"]),
        scalars=slab,
        held=t,
        scratch=[pltpu.VMEM((1024, 128), F32)],
    )
    got = exchange(send, "gz")
    out = air_finish_call(place, got, old, moved, drift, below, above)
    out = out.reshape(128, 2, LEVELS, 128).transpose(0, 2, 1, 3).reshape(tracer.shape)
    return new_rows, out


def solution(mesh):
    return jax.shard_map(
        shards,
        mesh=mesh,
        in_specs=(P(BOTH, None), P(BOTH, None), P("gx", "gz", None), P("gx", "gz", None)),
        out_specs=(P(BOTH, None), P("gx", "gz", None)),
        check_vma=False,
    )
```

profile of v0, /device:TPU:8, one launch (start us, length us, event | category | flops | bytes accessed | tf_op | source)
XLA Modules:
  0.0 161.0 jit_solution(1964831925215361847)
XLA Ops:
  0.6 2.5 %rows_start.1.refs_4_ = f32[256,128]{1,0:T(8,128)} custom-call(f32[16,2048]{1,0:T(8,128)} %refs_0_.2, bf16[2,256,256]{2,1,0:T(8,128)(2,1)} %constant.31.clone.refs_3_.refs_1_, f32[2,128,128]{2,1,0:T(8,128)} %constant.32.clone.refs_7_.refs_2_, bf16[2,256,128]{2,1,0:T(8,128)(2,1)} %constant.33.clone.refs_0_.refs_3_, ...), custom_call_target="tpu_custom_call" | custom-call | tf_op jit(solution)/shard_map/rows_start/pallas_call | solution.py:315
  3.2 10.5 %all-to-all-start = ((f32[128,2,128]{2,1,0:T(2,128)}), f32[128,2,128]{2,1,0:T(2,128)S(1)}, u32[]{:S(2)}, u32[]{:S(2)}) async-start(f32[128,2,128]{2,1,0:T(2,128)} %bitcast.48), calls=%async_computation | async-start | bytes 262144 | tf_op jit(solution)/shard_map/all_to_all | solution.py:683
  13.6 1.5 hold_tables.1
  15.1 7.7 %all-to-all-done = f32[128,2,128]{2,1,0:T(2,128)S(1)} async-done(((f32[128,2,128]{2,1,0:T(2,128)}), f32[128,2,128]{2,1,0:T(2,128)S(1)}, u32[]{:S(2)}, u32[]{:S(2)}) %all-to-all-start) | async-done | bytes 131104 | tf_op jit(solution)/shard_map/all_to_all | solution.py:683
  22.8 1.8 %shard_map.140 = (f32[256,128]{1,0:T(8,128)}, f32[512,128]{1,0:T(8,128)S(1)}) custom-call(s32[1]{0:T(128)} %bitcast.refs_0_, bf16[2,256,128]{2,1,0:T(8,128)(2,1)S(1)} %get-tuple-element.31.refs_1_, bf16[2,256,128]{2,1,0:T(8,128)(2,1)S(1)} %get-tuple-element.34.refs_2_, f32[2,128,128]{2,1,0:T(8,128)S(1)} %get-tuple-element.35.refs_3_, f32[256,128]{1,0:T(8,128)S(1)} %bitcast.44), custom_call_target="tpu_custom_call" | custom-call | tf_op jit(solution)/shard_map/pallas_call | solution.py:274
  24.6 4.8 %all-to-all-start.1 = ((f32[128,2,128]{2,1,0:T(2,128)}), f32[128,2,128]{2,1,0:T(2,128)S(1)}, u32[]{:S(2)}, u32[]{:S(2)}) async-start(f32[128,2,128]{2,1,0:T(2,128)} %bitcast.3), calls=%async_computation.1 | async-start | bytes 262144 | tf_op jit(solution)/shard_map/all_to_all | solution.py:683
  29.4 2.2 %shard_map.141 = (f32[256,128]{1,0:T(8,128)S(1)}, f32[128,256]{1,0:T(8,128)S(1)}, f32[256,128]{1,0:T(8,128)}, f32[32,128]{1,0:T(8,128)}) custom-call(bf16[2,256,256]{2,1,0:T(8,128)(2,1)S(1)} %get-tuple-element.36.refs_0_, bf16[2,256,128]{2,1,0:T(8,128)(2,1)S(1)} %get-tuple-element.31.refs_1_, bf16[2,256,256]{2,1,0:T(8,128)(2,1)S(1)} %get-tuple-element.37.refs_2_, ...), custom_call_target="tpu_custom_call" | custom-call | tf_op jit(solution)/shard_map/pallas_call | solution.py:274
  31.6 7.1 %all-to-all-done.1 = f32[128,2,128]{2,1,0:T(2,128)S(1)} async-done(((f32[128,2,128]{2,1,0:T(2,128)}), f32[128,2,128]{2,1,0:T(2,128)S(1)}, u32[]{:S(2)}, u32[]{:S(2)}) %all-to-all-start.1) | async-done | bytes 131104 | tf_op jit(solution)/shard_map/all_to_all | solution.py:683
  38.7 1.7 %shard_map.142 = (f32[512,128]{1,0:T(8,128)}, f32[128,256]{1,0:T(8,128)S(1)}) custom-call(bf16[2,256,256]{2,1,0:T(8,128)(2,1)S(1)} %get-tuple-element.36.refs_0_, bf16[2,256,128]{2,1,0:T(8,128)(2,1)S(1)} %get-tuple-element.31.refs_1_, bf16[2,256,256]{2,1,0:T(8,128)(2,1)S(1)} %get-tuple-element.37.refs_2_, f32[2,128,128]{2,1,0:T(8,128)S(1)} %get-tuple-element.33.refs_3_, ...), custom_call_target="tpu_custom_call" | custom-call | tf_op jit(solution)/shard_map/pallas_call | solution.py:274
  40.4 4.8 %all-to-all-start.2 = ((f32[128,4,128]{2,1,0:T(4,128)}), f32[128,4,128]{2,1,0:T(4,128)S(1)}, u32[]{:S(2)}, u32[]{:S(2)}) async-start(f32[128,4,128]{2,1,0:T(4,128)} %bitcast.54), calls=%async_computation.2 | async-start | bytes 524288 | tf_op jit(solution)/shard_map/all_to_all | solution.py:683
  45.2 0.9 shard_map.143.refs_5_
  46.1 9.6 %all-to-all-done.2 = f32[128,4,128]{2,1,0:T(4,128)S(1)} async-done(((f32[128,4,128]{2,1,0:T(4,128)}), f32[128,4,128]{2,1,0:T(4,128)S(1)}, u32[]{:S(2)}, u32[]{:S(2)}) %all-to-all-start.2) | async-done | bytes 262176 | tf_op jit(solution)/shard_map/all_to_all | solution.py:683
  55.7 1.9 %shard_map.144 = (f32[1024,128]{1,0:T(8,128)}, f32[768,128]{1,0:T(8,128)S(1)}) custom-call(s32[1]{0:T(128)} %bitcast.refs_0_, bf16[2,256,128]{2,1,0:T(8,128)(2,1)S(1)} %get-tuple-element.31.refs_1_, bf16[2,256,128]{2,1,0:T(8,128)(2,1)S(1)} %get-tuple-element.34.refs_2_, f32[2,128,128]{2,1,0:T(8,128)S(1)} %get-tuple-element.35.refs_3_, ...), custom_call_target="tpu_custom_call" | custom-call | tf_op jit(solution)/shard_map/pallas_call | solution.py:274
  57.6 18.2 %all_to_all.82 = f32[128,8,128]{2,1,0:T(8,128)S(1)} all-to-all(f32[128,8,128]{2,1,0:T(8,128)} %bitcast.53), channel_id=1, replica_groups=mesh['gx'=16,'gz'=8] {'gx','gz'}, dimensions={0} | all-to-all | bytes 1048576 | tf_op jit(solution)/shard_map/all_to_all | solution.py:683
  75.8 1.9 %shard_map.145 = (f32[256,128]{1,0:T(8,128)}, f32[128,256]{1,0:T(8,128)S(1)}, f32[128,256]{1,0:T(8,128)S(1)}) custom-call(bf16[2,256,256]{2,1,0:T(8,128)(2,1)S(1)} %get-tuple-element.36.refs_0_, bf16[2,256,128]{2,1,0:T(8,128)(2,1)S(1)} %get-tuple-element.31.refs_1_, bf16[2,256,256]{2,1,0:T(8,128)(2,1)S(1)} %get-tuple-element.37.refs_2_, ...), custom_call_target="tpu_custom_call" | custom-call | tf_op jit(solution)/shard_map/pallas_call | solution.py:274
  77.7 4.7 %all-to-all-start.4 = ((f32[128,2,128]{2,1,0:T(2,128)}), f32[128,2,128]{2,1,0:T(2,128)S(1)}, u32[]{:S(2)}, u32[]{:S(2)}) async-start(f32[128,2,128]{2,1,0:T(2,128)} %bitcast.55), calls=%async_computation.4 | async-start | bytes 262144 | tf_op jit(solution)/shard_map/all_to_all | solution.py:683
  82.5 1.2 shard_map.146.refs_5_
  83.7 8.1 %all-to-all-done.4 = f32[128,2,128]{2,1,0:T(2,128)S(1)} async-done(((f32[128,2,128]{2,1,0:T(2,128)}), f32[128,2,128]{2,1,0:T(2,128)S(1)}, u32[]{:S(2)}, u32[]{:S(2)}) %all-to-all-start.4) | async-done | bytes 131104 | tf_op jit(solution)/shard_map/all_to_all | solution.py:683
  91.8 1.8 %shard_map.147 = f32[768,128]{1,0:T(8,128)} custom-call(s32[1]{0:T(128)} %bitcast.refs_0_, bf16[2,256,128]{2,1,0:T(8,128)(2,1)S(1)} %get-tuple-element.31.refs_1_, bf16[2,256,128]{2,1,0:T(8,128)(2,1)S(1)} %get-tuple-element.34.refs_2_, f32[2,128,128]{2,1,0:T(8,128)S(1)} %get-tuple-element.35.refs_3_, f32[256,128]{1,0:T(8,128)S(1)} %bitcast.45, ...), custom_call_target="tpu_custom_call" | custom-call | tf_op jit(solution)/shard_map/pallas_call | solution.py:274
  93.6 4.9 %all-to-all-start.5 = ((f32[128,3,2,128]{3,2,1,0:T(2,128)}), f32[128,3,2,128]{3,2,1,0:T(2,128)S(1)}, u32[]{:S(2)}, u32[]{:S(2)}) async-start(f32[128,3,2,128]{3,2,1,0:T(2,128)} %bitcast.47), calls=%async_computation.5 | async-start | bytes 786432 | tf_op jit(solution)/shard_map/all_to_all | solution.py:683
  98.6 3.8 %collective-permute-start = (f32[32,128]{1,0:T(8,128)S(1)}, f32[32,128]{1,0:T(8,128)S(1)}, u32[]{:S(2)}, u32[]{:S(2)}) collective-permute-start(f32[32,128]{1,0:T(8,128)S(1)} %copy-done.5), channel_id=1, source_target_pairs={{0,1},{1,0},{2,3},{3,2},{4,5},{5,4},{6,7},{7,6},{8,9},{9,8},{10,11... | collective-permute-start | bytes 49160 | tf_op jit(solution)/shard_map/ppermute | solution.py:721
  102.3 1.8 %shard_map.149.refs_7_ = f32[256,256]{1,0:T(8,128)S(1)} custom-call(bf16[2,256,256]{2,1,0:T(8,128)(2,1)S(1)} %get-tuple-element.30.refs_4_.refs_0_, bf16[2,256,128]{2,1,0:T(8,128)(2,1)S(1)} %get-tuple-element.31.refs_1_, bf16[2,256,256]{2,1,0:T(8,128)(2,1)S(1)} %get-tuple-element.32.refs_5_.refs_2_, f32[2,128,128]{2,1,0:T(8,128)S(1)} %get-tuple-element.33.refs_3_, ...), custom_call_target="tpu_custom_call" | custom-call | tf_op jit(solution)/shard_map/pallas_call | solution.py:274
  104.1 0.8 shard_map.148.refs_6_
  104.9 5.5 %all-to-all-done.5 = f32[128,3,2,128]{3,2,1,0:T(2,128)S(1)} async-done(((f32[128,3,2,128]{3,2,1,0:T(2,128)}), f32[128,3,2,128]{3,2,1,0:T(2,128)S(1)}, u32[]{:S(2)}, u32[]{:S(2)}) %all-to-all-start.5) | async-done | bytes 393248 | tf_op jit(solution)/shard_map/all_to_all | solution.py:683
  110.4 1.6 %shard_map.150 = (f32[16,2048]{1,0:T(8,128)S(1)}, f32[512,128]{1,0:T(8,128)}, f32[32,128]{1,0:T(8,128)S(1)}) custom-call(bf16[2,256,256]{2,1,0:T(8,128)(2,1)S(1)} %get-tuple-element.30.refs_4_.refs_0_, bf16[2,256,128]{2,1,0:T(8,128)(2,1)S(1)} %get-tuple-element.31.refs_1_, bf16[2,256,256]{2,1,0:T(8,128)(2,1)S(1)} %get-tuple-element.32.refs_5_.refs_2_, ...), custom_call_target="tpu_custom_call" | custom-call | tf_op jit(solution)/shard_map/pallas_call | solution.py:274
  112.0 4.7 %all-to-all-start.6 = ((f32[128,4,128]{2,1,0:T(4,128)}), f32[128,4,128]{2,1,0:T(4,128)S(1)}, u32[]{:S(2)}, u32[]{:S(2)}) async-start(f32[128,4,128]{2,1,0:T(4,128)} %bitcast.15), calls=%async_computation.6 | async-start | bytes 524288 | tf_op jit(solution)/shard_map/all_to_all | solution.py:683
  116.8 0.7 slice_bitcast_fusion
  117.5 3.6 %collective-permute-start.4 = (f32[16,128]{1,0:T(8,128)S(1)}, f32[16,128]{1,0:T(8,128)S(1)}, u32[]{:S(2)}, u32[]{:S(2)}) collective-permute-start(f32[16,128]{1,0:T(8,128)S(1)} %get-tuple-element.58), channel_id=1, source_target_pairs={{8,0},{16,8},{24,16},{32,24},{40,32},{48,40},{56,48},{64,56},{72,6... | collective-permute-start | bytes 24584 | tf_op jit(solution)/shard_map/ppermute | solution.py:717
  121.1 0.0 collective-permute-start.3
  121.1 0.6 pad_maximum_fusion.2
  121.8 0.5 collective-permute-start.1
  122.3 0.1 pad_add_fusion.place
  122.3 0.2 collective-permute-done.4.after
  122.5 3.8 %collective-permute-done.3.before = f32[16,128]{1,0:T(8,128)S(1)} collective-permute-done((f32[16,128]{1,0:T(8,128)S(1)}, f32[16,128]{1,0:T(8,128)S(1)}, u32[]{:S(2)}, u32[]{:S(2)}) %collective-permute-start.3) | collective-permute-done | bytes 8224 | tf_op jit(solution)/shard_map/ppermute | solution.py:716
  126.3 0.6 copy-done.10
  126.9 5.5 %air_moved.1 = (f32[2048,128]{1,0:T(8,128)}, f32[2048,128]{1,0:T(8,128)}, f32[512,128]{1,0:T(8,128)}, f32[512,128]{1,0:T(8,128)}) custom-call(s32[2]{0:T(128)S(1)} %pad_add_fusion.place, f32[2048,128]{1,0:T(8,128)} %bitcast.50, f32[2048,128]{1,0:T(8,128)} %bitcast.51, f32[16,128]{1,0:T(8,128)} %copy-done.10, f32[16,128]{1,0:T(8,128)} %copy-done.9), custom_call_target="tpu_custom_call" | custom-call | tf_op jit(solution)/shard_map/air_moved/pallas_call | solution.py:644
  132.4 5.1 %collective-permute-start.5 = (f32[512,128]{1,0:T(8,128)}, f32[512,128]{1,0:T(8,128)}, u32[]{:S(2)}, u32[]{:S(2)}) collective-permute-start(f32[512,128]{1,0:T(8,128)} %get-tuple-element.56), channel_id=1, source_target_pairs={{0,1},{1,2},{2,3},{3,4},{4,5},{5,6},{6,7},{8,9},{9,10},{10,11},{11... | collective-permute-start | bytes 786440 | tf_op jit(solution)/shard_map/ppermute | solution.py:738
  137.5 3.1 %collective-permute-start.6 = (f32[512,128]{1,0:T(8,128)}, f32[512,128]{1,0:T(8,128)}, u32[]{:S(2)}, u32[]{:S(2)}) collective-permute-start(f32[512,128]{1,0:T(8,128)} %get-tuple-element.57), channel_id=1, source_target_pairs={{1,0},{2,1},{3,2},{4,3},{5,4},{6,5},{7,6},{9,8},{10,9},{11,10},{12... | collective-permute-start | bytes 786440 | tf_op jit(solution)/shard_map/ppermute | solution.py:739
  140.7 0.0 copy-start.1
  140.7 1.4 shard_map.151
  142.1 7.2 %all-to-all-start.7 = ((f32[8,64,128]{2,1,0:T(8,128)}), f32[8,64,128]{2,1,0:T(8,128)S(1)}, u32[]{:S(2)}, u32[]{:S(2)}) async-start(f32[8,64,128]{2,1,0:T(8,128)} %bitcast.17), calls=%async_computation.7 | async-start | bytes 524288 | tf_op jit(solution)/shard_map/all_to_all | solution.py:683
  149.3 0.8 pad_maximum_fusion.1
  150.1 2.1 %collective-permute-start.2 = (f32[128,128]{1,0:T(8,128)S(1)}, f32[128,128]{1,0:T(8,128)S(1)}, u32[]{:S(2)}, u32[]{:S(2)}) collective-permute-start(f32[128,128]{1,0:T(8,128)S(1)} %pad_maximum_fusion.1), channel_id=1, source_target_pairs={{0,4},{1,5},{2,6},{3,7},{4,0},{5,1},{6,2},{7,3},{8,12},{9,13},{10,... | collective-permute-start | bytes 196616 | tf_op jit(solution)/shard_map/ppermute | solution.py:721
  152.1 3.7 %collective-permute-done.2 = f32[128,128]{1,0:T(8,128)S(1)} collective-permute-done((f32[128,128]{1,0:T(8,128)S(1)}, f32[128,128]{1,0:T(8,128)S(1)}, u32[]{:S(2)}, u32[]{:S(2)}) %collective-permute-start.2) | collective-permute-done | bytes 65568 | tf_op jit(solution)/shard_map/ppermute | solution.py:721
  155.8 0.8 pad_maximum_fusion.before
  156.6 0.7 copy.15
  157.3 0.6 copy-done.4
  158.0 2.9 %air_finish.1 = f32[2048,128]{1,0:T(8,128)} custom-call(s32[2]{0:T(128)S(1)} %copy-done.4, f32[512,128]{1,0:T(8,128)S(1)} %bitcast.41, f32[256,128]{1,0:T(8,128)S(1)} %pad_maximum_fusion.before, f32[2048,128]{1,0:T(8,128)S(1)} %copy-done.1, f32[2048,128]{1,0:T(8,128)S(1)} %copy-done.2, f32[512,128]{1,0:T(8,128)} %collective-permute-done.5.below, ...), custom_call_target="tpu_custom_call" | custom-call | tf_op jit(solution)/shard_map/air_finish/pallas_call | solution.py:664
  (25 shorter events, 0.1 us)
Async XLA Ops:
  3.2 19.7 %all-to-all-start = ((f32[128,2,128]{2,1,0:T(2,128)}), f32[128,2,128]{2,1,0:T(2,128)S(1)}, u32[]{:S(2)}, u32[]{:S(2)}) async-start(f32[128,2,128]{2,1,0:T(2,128)} %bitcast.48), calls=%async_computation | async-start | bytes 262144 | tf_op jit(solution)/shard_map/all_to_all | solution.py:683
  24.6 14.1 %all-to-all-start.1 = ((f32[128,2,128]{2,1,0:T(2,128)}), f32[128,2,128]{2,1,0:T(2,128)S(1)}, u32[]{:S(2)}, u32[]{:S(2)}) async-start(f32[128,2,128]{2,1,0:T(2,128)} %bitcast.3), calls=%async_computation.1 | async-start | bytes 262144 | tf_op jit(solution)/shard_map/all_to_all | solution.py:683
  40.4 15.3 %all-to-all-start.2 = ((f32[128,4,128]{2,1,0:T(4,128)}), f32[128,4,128]{2,1,0:T(4,128)S(1)}, u32[]{:S(2)}, u32[]{:S(2)}) async-start(f32[128,4,128]{2,1,0:T(4,128)} %bitcast.54), calls=%async_computation.2 | async-start | bytes 524288 | tf_op jit(solution)/shard_map/all_to_all | solution.py:683
  77.7 14.1 %all-to-all-start.4 = ((f32[128,2,128]{2,1,0:T(2,128)}), f32[128,2,128]{2,1,0:T(2,128)S(1)}, u32[]{:S(2)}, u32[]{:S(2)}) async-start(f32[128,2,128]{2,1,0:T(2,128)} %bitcast.55), calls=%async_computation.4 | async-start | bytes 262144 | tf_op jit(solution)/shard_map/all_to_all | solution.py:683
  93.6 4.9 %copy-start.5 = (f32[32,128]{1,0:T(8,128)S(1)}, f32[32,128]{1,0:T(8,128)}, u32[]{:S(2)}) copy-start(f32[32,128]{1,0:T(8,128)} %get-tuple-element.53) | copy-start | bytes 49156
  93.6 16.8 %all-to-all-start.5 = ((f32[128,3,2,128]{3,2,1,0:T(2,128)}), f32[128,3,2,128]{3,2,1,0:T(2,128)S(1)}, u32[]{:S(2)}, u32[]{:S(2)}) async-start(f32[128,3,2,128]{3,2,1,0:T(2,128)} %bitcast.47), calls=%async_computation.5 | async-start | bytes 786432 | tf_op jit(solution)/shard_map/all_to_all | solution.py:683
  98.6 22.6 %collective-permute-start = (f32[32,128]{1,0:T(8,128)S(1)}, f32[32,128]{1,0:T(8,128)S(1)}, u32[]{:S(2)}, u32[]{:S(2)}) collective-permute-start(f32[32,128]{1,0:T(8,128)S(1)} %copy-done.5), channel_id=1, source_target_pairs={{0,1},{1,0},{2,3},{3,2},{4,5},{5,4},{6,7},{7,6},{8,9},{9,8},{10,11... | collective-permute-start | bytes 49160 | tf_op jit(solution)/shard_map/ppermute | solution.py:721
  112.0 28.6 %all-to-all-start.6 = ((f32[128,4,128]{2,1,0:T(4,128)}), f32[128,4,128]{2,1,0:T(4,128)S(1)}, u32[]{:S(2)}, u32[]{:S(2)}) async-start(f32[128,4,128]{2,1,0:T(4,128)} %bitcast.15), calls=%async_computation.6 | async-start | bytes 524288 | tf_op jit(solution)/shard_map/all_to_all | solution.py:683
  117.5 5.0 %collective-permute-start.4 = (f32[16,128]{1,0:T(8,128)S(1)}, f32[16,128]{1,0:T(8,128)S(1)}, u32[]{:S(2)}, u32[]{:S(2)}) collective-permute-start(f32[16,128]{1,0:T(8,128)S(1)} %get-tuple-element.58), channel_id=1, source_target_pairs={{8,0},{16,8},{24,16},{32,24},{40,32},{48,40},{56,48},{64,56},{72,6... | collective-permute-start | bytes 24584 | tf_op jit(solution)/shard_map/ppermute | solution.py:717
  121.1 5.2 %collective-permute-start.3 = (f32[16,128]{1,0:T(8,128)S(1)}, f32[16,128]{1,0:T(8,128)S(1)}, u32[]{:S(2)}, u32[]{:S(2)}) collective-permute-start(f32[16,128]{1,0:T(8,128)S(1)} %get-tuple-element.59), channel_id=1, source_target_pairs={{0,8},{8,16},{16,24},{24,32},{32,40},{40,48},{48,56},{56,64},{64,7... | collective-permute-start | bytes 24584 | tf_op jit(solution)/shard_map/ppermute | solution.py:716
  121.1 11.3 %copy-start.7 = (f32[32,128]{1,0:T(8,128)}, f32[32,128]{1,0:T(8,128)S(1)}, u32[]{:S(2)}) copy-start(f32[32,128]{1,0:T(8,128)S(1)} %collective-permute-done) | copy-start | bytes 49156
  121.8 27.5 %collective-permute-start.1 = (f32[64,128]{1,0:T(8,128)}, f32[64,128]{1,0:T(8,128)}, u32[]{:S(2)}, u32[]{:S(2)}) collective-permute-start(f32[64,128]{1,0:T(8,128)} %pad_maximum_fusion.2), channel_id=1, source_target_pairs={{0,2},{1,3},{2,0},{3,1},{4,6},{5,7},{6,4},{7,5},{8,10},{9,11},{10,... | collective-permute-start | bytes 98312 | tf_op jit(solution)/shard_map/ppermute | solution.py:721
  122.3 4.0 %copy-start.3 = (s32[2]{0:T(128)}, s32[2]{0:T(128)S(1)}, u32[]{:S(2)}) copy-start(s32[2]{0:T(128)S(1)} %pad_add_fusion.place) | copy-start | bytes 28
  122.5 3.8 %copy-start.9 = (f32[16,128]{1,0:T(8,128)}, f32[16,128]{1,0:T(8,128)S(1)}, u32[]{:S(2)}) copy-start(f32[16,128]{1,0:T(8,128)S(1)} %collective-permute-done.4.after) | copy-start | bytes 24580
  126.3 0.6 copy-start.10
  126.9 13.8 %copy-start = (bf16[2,512,512]{2,1,0:T(8,128)(2,1)S(1)}, bf16[2,512,512]{2,1,0:T(8,128)(2,1)}, u32[]{:S(2)}) copy-start(bf16[2,512,512]{2,1,0:T(8,128)(2,1)} %constant.39.clone.refs_3_) | copy-start | bytes 3145732
  132.4 24.9 %collective-permute-start.5 = (f32[512,128]{1,0:T(8,128)}, f32[512,128]{1,0:T(8,128)}, u32[]{:S(2)}, u32[]{:S(2)}) collective-permute-start(f32[512,128]{1,0:T(8,128)} %get-tuple-element.56), channel_id=1, source_target_pairs={{0,1},{1,2},{2,3},{3,4},{4,5},{5,6},{6,7},{8,9},{9,10},{10,11},{11... | collective-permute-start | bytes 786440 | tf_op jit(solution)/shard_map/ppermute | solution.py:738
  137.5 19.7 %collective-permute-start.6 = (f32[512,128]{1,0:T(8,128)}, f32[512,128]{1,0:T(8,128)}, u32[]{:S(2)}, u32[]{:S(2)}) collective-permute-start(f32[512,128]{1,0:T(8,128)} %get-tuple-element.57), channel_id=1, source_target_pairs={{1,0},{2,1},{3,2},{4,3},{5,4},{6,5},{7,6},{9,8},{10,9},{11,10},{12... | collective-permute-start | bytes 786440 | tf_op jit(solution)/shard_map/ppermute | solution.py:739
  140.7 16.6 %copy-start.1 = (f32[2048,128]{1,0:T(8,128)S(1)}, f32[2048,128]{1,0:T(8,128)}, u32[]{:S(2)}) copy-start(f32[2048,128]{1,0:T(8,128)} %get-tuple-element.54.moved) | copy-start | bytes 3145732
  140.7 16.6 %copy-start.2 = (f32[2048,128]{1,0:T(8,128)S(1)}, f32[2048,128]{1,0:T(8,128)}, u32[]{:S(2)}) copy-start(f32[2048,128]{1,0:T(8,128)} %get-tuple-element.55.drift) | copy-start | bytes 3145732
  142.1 7.2 %copy-start.6 = (f32[32,128]{1,0:T(8,128)S(1)}, f32[32,128]{1,0:T(8,128)}, u32[]{:S(2)}) copy-start(f32[32,128]{1,0:T(8,128)} %get-tuple-element.53) | copy-start | bytes 49156
  142.1 15.2 %all-to-all-start.7 = ((f32[8,64,128]{2,1,0:T(8,128)}), f32[8,64,128]{2,1,0:T(8,128)S(1)}, u32[]{:S(2)}, u32[]{:S(2)}) async-start(f32[8,64,128]{2,1,0:T(8,128)} %bitcast.17), calls=%async_computation.7 | async-start | bytes 524288 | tf_op jit(solution)/shard_map/all_to_all | solution.py:683
  149.3 6.6 %copy-start.8 = (f32[32,128]{1,0:T(8,128)S(1)}, f32[32,128]{1,0:T(8,128)}, u32[]{:S(2)}) copy-start(f32[32,128]{1,0:T(8,128)} %copy-done.7) | copy-start | bytes 49156
  150.1 5.8 %collective-permute-start.2 = (f32[128,128]{1,0:T(8,128)S(1)}, f32[128,128]{1,0:T(8,128)S(1)}, u32[]{:S(2)}, u32[]{:S(2)}) collective-permute-start(f32[128,128]{1,0:T(8,128)S(1)} %pad_maximum_fusion.1), channel_id=1, source_target_pairs={{0,4},{1,5},{2,6},{3,7},{4,0},{5,1},{6,2},{7,3},{8,12},{9,13},{10,... | collective-permute-start | bytes 196616 | tf_op jit(solution)/shard_map/ppermute | solution.py:721
  157.3 0.7 copy-start.4
where the time goes:
time: 162 us; the launch traced here: 161 us
  starting transfers between devices  59.8 us (37%)
  waiting for transfers between devices  45.8 us (28%)
  Pallas kernels  31.3 us (19%)
  blocking collectives  18.2 us (11%)
  local copies, waits for them, and re-layouts  2.65 us (2%)
  other arithmetic  2.24 us (1%)
    all_to_all x7, starting transfers between devices, exchange(): out = lax.all_to_all(buffer, axes, split_axis=0, concat_axis=0, tiled=True)  41.6 us
    all_to_all x7, waiting for transfers between devices, exchange(): out = lax.all_to_all(buffer, axes, split_axis=0, concat_axis=0, tiled=True)  38.1 us
    pallas_call x12, Pallas kernels, run(): pl.pallas_call(kernel, out_shape=[place(out) for out in outs], in_specs=[...  19 us
    all_to_all x1, blocking collectives, exchange(): out = lax.all_to_all(buffer, axes, split_axis=0, concat_axis=0, tiled=True)  18.2 us
    ppermute x3, starting transfers between devices, shards(): old = jnp.concatenate([old, lax.ppermute(old, 'gz', pairs)], 0)  6.33 us
    pallas_call x1, Pallas kernels, air_moved_call(): pl.pallas_call(air_moved, out_shape=[pltpu.HBM((2048, 128), F32)] * 2 + [...  5.47 us
    ppermute x1, starting transfers between devices, shards(): below = lax.ppermute(top, 'gz', rise)  5.12 us
    ppermute x1, waiting for transfers between devices, shards(): before = lax.ppermute(quantity[-16:], 'gx', ring)  3.82 us
  transfers between devices with their start and end apart: 14, of which 8 were waited for; matrix products, arithmetic and copies ran while one was open for 2% of the time, Pallas kernels for 10%

commit v1 on v0

--- a/solution.py
+++ b/solution.py
@@ -629,10 +629,10 @@
         return carry
 
     copies = []
-    for quarter in range(4):
-        lax.fori_loop(4 * quarter, 4 * quarter + 4, step, 0)
-        rows = pl.ds(512 * quarter, 512)
-        copies.append(pltpu.make_async_copy(out_s.at[rows], out.at[rows], sems.at[quarter]))
+    for part in range(8):
+        lax.fori_loop(2 * part, 2 * part + 2, step, 0)
+        rows = pl.ds(256 * part, 256)
+        copies.append(pltpu.make_async_copy(out_s.at[rows], out.at[rows], sems.at[part]))
         copies[-1].start()
     for copy in copies:
         copy.wait()
@@ -667,7 +667,7 @@
         in_specs=[pl.BlockSpec(memory_space=pltpu.SMEM)] + [vmem] * 6,
         out_specs=pl.BlockSpec(memory_space=pltpu.HBM),
         scratch_shapes=[pltpu.VMEM((128, 256), F32)] * 4
-        + [pltpu.VMEM((2048, 128), F32), pltpu.SemaphoreType.DMA((4,))],
+        + [pltpu.VMEM((2048, 128), F32), pltpu.SemaphoreType.DMA((8,))],
         compiler_params=pltpu.CompilerParams(vmem_limit_bytes=16 << 20),
         name="air_finish",
     )(place, *near)

time: 162 us -> 162 us (level)
  no operation moved by 1% of the time
where the time goes in v1:
time: 162 us; the launch traced here: 161 us
  starting transfers between devices  59.8 us (37%)
  waiting for transfers between devices  45.8 us (28%)
  Pallas kernels  31.3 us (19%)
  blocking collectives  18.2 us (11%)
  local copies, waits for them, and re-layouts  2.65 us (2%)
  other arithmetic  2.24 us (1%)
    all_to_all x7, starting transfers between devices, exchange(): out = lax.all_to_all(buffer, axes, split_axis=0, concat_axis=0, tiled=True)  41.6 us
    all_to_all x7, waiting for transfers between devices, exchange(): out = lax.all_to_all(buffer, axes, split_axis=0, concat_axis=0, tiled=True)  38.1 us
    pallas_call x12, Pallas kernels, run(): pl.pallas_call(kernel, out_shape=[place(out) for out in outs], in_specs=[...  19 us
    all_to_all x1, blocking collectives, exchange(): out = lax.all_to_all(buffer, axes, split_axis=0, concat_axis=0, tiled=True)  18.2 us
    ppermute x3, starting transfers between devices, shards(): old = jnp.concatenate([old, lax.ppermute(old, 'gz', pairs)], 0)  6.33 us
    pallas_call x1, Pallas kernels, air_moved_call(): pl.pallas_call(air_moved, out_shape=[pltpu.HBM((2048, 128), F32)] * 2 + [...  5.47 us
    ppermute x1, starting transfers between devices, shards(): below = lax.ppermute(top, 'gz', rise)  5.12 us
    ppermute x1, waiting for transfers between devices, shards(): before = lax.ppermute(quantity[-16:], 'gx', ring)  3.82 us
  transfers between devices with their start and end apart: 14, of which 8 were waited for; matrix products, arithmetic and copies ran while one was open for 2% of the time, Pallas kernels for 10%

profile of v1, /device:TPU:8, one launch (start us, length us, event | category | flops | bytes accessed | tf_op | source)
XLA Modules:
  0.0 161.0 jit_solution(8778987202110965511)
XLA Ops:
  0.6 2.5 %rows_start.1.refs_4_ = f32[256,128]{1,0:T(8,128)} custom-call(f32[16,2048]{1,0:T(8,128)} %refs_0_.2, bf16[2,256,256]{2,1,0:T(8,128)(2,1)} %constant.31.clone.refs_3_.refs_1_, f32[2,128,128]{2,1,0:T(8,128)} %constant.32.clone.refs_7_.refs_2_, bf16[2,256,128]{2,1,0:T(8,128)(2,1)} %constant.33.clone.refs_0_.refs_3_, ...), custom_call_target="tpu_custom_call" | custom-call | tf_op jit(solution)/shard_map/rows_start/pallas_call | solution.py:315
  3.2 10.5 %all-to-all-start = ((f32[128,2,128]{2,1,0:T(2,128)}), f32[128,2,128]{2,1,0:T(2,128)S(1)}, u32[]{:S(2)}, u32[]{:S(2)}) async-start(f32[128,2,128]{2,1,0:T(2,128)} %bitcast.48), calls=%async_computation | async-start | bytes 262144 | tf_op jit(solution)/shard_map/all_to_all | solution.py:683
  13.6 1.5 hold_tables.1
  15.1 7.7 %all-to-all-done = f32[128,2,128]{2,1,0:T(2,128)S(1)} async-done(((f32[128,2,128]{2,1,0:T(2,128)}), f32[128,2,128]{2,1,0:T(2,128)S(1)}, u32[]{:S(2)}, u32[]{:S(2)}) %all-to-all-start) | async-done | bytes 131104 | tf_op jit(solution)/shard_map/all_to_all | solution.py:683
  22.8 1.8 %shard_map.140 = (f32[256,128]{1,0:T(8,128)}, f32[512,128]{1,0:T(8,128)S(1)}) custom-call(s32[1]{0:T(128)} %bitcast.refs_0_, bf16[2,256,128]{2,1,0:T(8,128)(2,1)S(1)} %get-tuple-element.31.refs_1_, bf16[2,256,128]{2,1,0:T(8,128)(2,1)S(1)} %get-tuple-element.34.refs_2_, f32[2,128,128]{2,1,0:T(8,128)S(1)} %get-tuple-element.35.refs_3_, f32[256,128]{1,0:T(8,128)S(1)} %bitcast.44), custom_call_target="tpu_custom_call" | custom-call | tf_op jit(solution)/shard_map/pallas_call | solution.py:274
  24.6 4.8 %all-to-all-start.1 = ((f32[128,2,128]{2,1,0:T(2,128)}), f32[128,2,128]{2,1,0:T(2,128)S(1)}, u32[]{:S(2)}, u32[]{:S(2)}) async-start(f32[128,2,128]{2,1,0:T(2,128)} %bitcast.3), calls=%async_computation.1 | async-start | bytes 262144 | tf_op jit(solution)/shard_map/all_to_all | solution.py:683
  29.4 2.2 %shard_map.141 = (f32[256,128]{1,0:T(8,128)S(1)}, f32[128,256]{1,0:T(8,128)S(1)}, f32[256,128]{1,0:T(8,128)}, f32[32,128]{1,0:T(8,128)}) custom-call(bf16[2,256,256]{2,1,0:T(8,128)(2,1)S(1)} %get-tuple-element.36.refs_0_, bf16[2,256,128]{2,1,0:T(8,128)(2,1)S(1)} %get-tuple-element.31.refs_1_, bf16[2,256,256]{2,1,0:T(8,128)(2,1)S(1)} %get-tuple-element.37.refs_2_, ...), custom_call_target="tpu_custom_call" | custom-call | tf_op jit(solution)/shard_map/pallas_call | solution.py:274
  31.6 7.1 %all-to-all-done.1 = f32[128,2,128]{2,1,0:T(2,128)S(1)} async-done(((f32[128,2,128]{2,1,0:T(2,128)}), f32[128,2,128]{2,1,0:T(2,128)S(1)}, u32[]{:S(2)}, u32[]{:S(2)}) %all-to-all-start.1) | async-done | bytes 131104 | tf_op jit(solution)/shard_map/all_to_all | solution.py:683
  38.7 1.7 %shard_map.142 = (f32[512,128]{1,0:T(8,128)}, f32[128,256]{1,0:T(8,128)S(1)}) custom-call(bf16[2,256,256]{2,1,0:T(8,128)(2,1)S(1)} %get-tuple-element.36.refs_0_, bf16[2,256,128]{2,1,0:T(8,128)(2,1)S(1)} %get-tuple-element.31.refs_1_, bf16[2,256,256]{2,1,0:T(8,128)(2,1)S(1)} %get-tuple-element.37.refs_2_, f32[2,128,128]{2,1,0:T(8,128)S(1)} %get-tuple-element.33.refs_3_, ...), custom_call_target="tpu_custom_call" | custom-call | tf_op jit(solution)/shard_map/pallas_call | solution.py:274
  40.4 4.8 %all-to-all-start.2 = ((f32[128,4,128]{2,1,0:T(4,128)}), f32[128,4,128]{2,1,0:T(4,128)S(1)}, u32[]{:S(2)}, u32[]{:S(2)}) async-start(f32[128,4,128]{2,1,0:T(4,128)} %bitcast.54), calls=%async_computation.2 | async-start | bytes 524288 | tf_op jit(solution)/shard_map/all_to_all | solution.py:683
  45.2 0.9 shard_map.143.refs_5_
  46.1 9.6 %all-to-all-done.2 = f32[128,4,128]{2,1,0:T(4,128)S(1)} async-done(((f32[128,4,128]{2,1,0:T(4,128)}), f32[128,4,128]{2,1,0:T(4,128)S(1)}, u32[]{:S(2)}, u32[]{:S(2)}) %all-to-all-start.2) | async-done | bytes 262176 | tf_op jit(solution)/shard_map/all_to_all | solution.py:683
  55.7 1.9 %shard_map.144 = (f32[1024,128]{1,0:T(8,128)}, f32[768,128]{1,0:T(8,128)S(1)}) custom-call(s32[1]{0:T(128)} %bitcast.refs_0_, bf16[2,256,128]{2,1,0:T(8,128)(2,1)S(1)} %get-tuple-element.31.refs_1_, bf16[2,256,128]{2,1,0:T(8,128)(2,1)S(1)} %get-tuple-element.34.refs_2_, f32[2,128,128]{2,1,0:T(8,128)S(1)} %get-tuple-element.35.refs_3_, ...), custom_call_target="tpu_custom_call" | custom-call | tf_op jit(solution)/shard_map/pallas_call | solution.py:274
  57.6 18.2 %all_to_all.82 = f32[128,8,128]{2,1,0:T(8,128)S(1)} all-to-all(f32[128,8,128]{2,1,0:T(8,128)} %bitcast.53), channel_id=1, replica_groups=mesh['gx'=16,'gz'=8] {'gx','gz'}, dimensions={0} | all-to-all | bytes 1048576 | tf_op jit(solution)/shard_map/all_to_all | solution.py:683
  75.8 1.9 %shard_map.145 = (f32[256,128]{1,0:T(8,128)}, f32[128,256]{1,0:T(8,128)S(1)}, f32[128,256]{1,0:T(8,128)S(1)}) custom-call(bf16[2,256,256]{2,1,0:T(8,128)(2,1)S(1)} %get-tuple-element.36.refs_0_, bf16[2,256,128]{2,1,0:T(8,128)(2,1)S(1)} %get-tuple-element.31.refs_1_, bf16[2,256,256]{2,1,0:T(8,128)(2,1)S(1)} %get-tuple-element.37.refs_2_, ...), custom_call_target="tpu_custom_call" | custom-call | tf_op jit(solution)/shard_map/pallas_call | solution.py:274
  77.7 4.7 %all-to-all-start.4 = ((f32[128,2,128]{2,1,0:T(2,128)}), f32[128,2,128]{2,1,0:T(2,128)S(1)}, u32[]{:S(2)}, u32[]{:S(2)}) async-start(f32[128,2,128]{2,1,0:T(2,128)} %bitcast.55), calls=%async_computation.4 | async-start | bytes 262144 | tf_op jit(solution)/shard_map/all_to_all | solution.py:683
  82.5 1.2 shard_map.146.refs_5_
  83.7 8.1 %all-to-all-done.4 = f32[128,2,128]{2,1,0:T(2,128)S(1)} async-done(((f32[128,2,128]{2,1,0:T(2,128)}), f32[128,2,128]{2,1,0:T(2,128)S(1)}, u32[]{:S(2)}, u32[]{:S(2)}) %all-to-all-start.4) | async-done | bytes 131104 | tf_op jit(solution)/shard_map/all_to_all | solution.py:683
  91.8 1.8 %shard_map.147 = f32[768,128]{1,0:T(8,128)} custom-call(s32[1]{0:T(128)} %bitcast.refs_0_, bf16[2,256,128]{2,1,0:T(8,128)(2,1)S(1)} %get-tuple-element.31.refs_1_, bf16[2,256,128]{2,1,0:T(8,128)(2,1)S(1)} %get-tuple-element.34.refs_2_, f32[2,128,128]{2,1,0:T(8,128)S(1)} %get-tuple-element.35.refs_3_, f32[256,128]{1,0:T(8,128)S(1)} %bitcast.45, ...), custom_call_target="tpu_custom_call" | custom-call | tf_op jit(solution)/shard_map/pallas_call | solution.py:274
  93.6 4.9 %all-to-all-start.5 = ((f32[128,3,2,128]{3,2,1,0:T(2,128)}), f32[128,3,2,128]{3,2,1,0:T(2,128)S(1)}, u32[]{:S(2)}, u32[]{:S(2)}) async-start(f32[128,3,2,128]{3,2,1,0:T(2,128)} %bitcast.47), calls=%async_computation.5 | async-start | bytes 786432 | tf_op jit(solution)/shard_map/all_to_all | solution.py:683
  98.6 3.8 %collective-permute-start = (f32[32,128]{1,0:T(8,128)S(1)}, f32[32,128]{1,0:T(8,128)S(1)}, u32[]{:S(2)}, u32[]{:S(2)}) collective-permute-start(f32[32,128]{1,0:T(8,128)S(1)} %copy-done.5), channel_id=1, source_target_pairs={{0,1},{1,0},{2,3},{3,2},{4,5},{5,4},{6,7},{7,6},{8,9},{9,8},{10,11... | collective-permute-start | bytes 49160 | tf_op jit(solution)/shard_map/ppermute | solution.py:721
  102.3 1.8 %shard_map.149.refs_7_ = f32[256,256]{1,0:T(8,128)S(1)} custom-call(bf16[2,256,256]{2,1,0:T(8,128)(2,1)S(1)} %get-tuple-element.30.refs_4_.refs_0_, bf16[2,256,128]{2,1,0:T(8,128)(2,1)S(1)} %get-tuple-element.31.refs_1_, bf16[2,256,256]{2,1,0:T(8,128)(2,1)S(1)} %get-tuple-element.32.refs_5_.refs_2_, f32[2,128,128]{2,1,0:T(8,128)S(1)} %get-tuple-element.33.refs_3_, ...), custom_call_target="tpu_custom_call" | custom-call | tf_op jit(solution)/shard_map/pallas_call | solution.py:274
  104.1 0.8 shard_map.148.refs_6_
  104.9 5.5 %all-to-all-done.5 = f32[128,3,2,128]{3,2,1,0:T(2,128)S(1)} async-done(((f32[128,3,2,128]{3,2,1,0:T(2,128)}), f32[128,3,2,128]{3,2,1,0:T(2,128)S(1)}, u32[]{:S(2)}, u32[]{:S(2)}) %all-to-all-start.5) | async-done | bytes 393248 | tf_op jit(solution)/shard_map/all_to_all | solution.py:683
  110.4 1.6 %shard_map.150 = (f32[16,2048]{1,0:T(8,128)S(1)}, f32[512,128]{1,0:T(8,128)}, f32[32,128]{1,0:T(8,128)S(1)}) custom-call(bf16[2,256,256]{2,1,0:T(8,128)(2,1)S(1)} %get-tuple-element.30.refs_4_.refs_0_, bf16[2,256,128]{2,1,0:T(8,128)(2,1)S(1)} %get-tuple-element.31.refs_1_, bf16[2,256,256]{2,1,0:T(8,128)(2,1)S(1)} %get-tuple-element.32.refs_5_.refs_2_, ...), custom_call_target="tpu_custom_call" | custom-call | tf_op jit(solution)/shard_map/pallas_call | solution.py:274
  112.0 4.7 %all-to-all-start.6 = ((f32[128,4,128]{2,1,0:T(4,128)}), f32[128,4,128]{2,1,0:T(4,128)S(1)}, u32[]{:S(2)}, u32[]{:S(2)}) async-start(f32[128,4,128]{2,1,0:T(4,128)} %bitcast.15), calls=%async_computation.6 | async-start | bytes 524288 | tf_op jit(solution)/shard_map/all_to_all | solution.py:683
  116.8 0.7 slice_bitcast_fusion
  117.5 3.6 %collective-permute-start.4 = (f32[16,128]{1,0:T(8,128)S(1)}, f32[16,128]{1,0:T(8,128)S(1)}, u32[]{:S(2)}, u32[]{:S(2)}) collective-permute-start(f32[16,128]{1,0:T(8,128)S(1)} %get-tuple-element.58), channel_id=1, source_target_pairs={{8,0},{16,8},{24,16},{32,24},{40,32},{48,40},{56,48},{64,56},{72,6... | collective-permute-start | bytes 24584 | tf_op jit(solution)/shard_map/ppermute | solution.py:717
  121.1 0.0 collective-permute-start.3
  121.1 0.6 pad_maximum_fusion.2
  121.8 0.5 collective-permute-start.1
  122.3 0.1 pad_add_fusion.place
  122.3 0.2 collective-permute-done.4.after
  122.5 3.8 %collective-permute-done.3.before = f32[16,128]{1,0:T(8,128)S(1)} collective-permute-done((f32[16,128]{1,0:T(8,128)S(1)}, f32[16,128]{1,0:T(8,128)S(1)}, u32[]{:S(2)}, u32[]{:S(2)}) %collective-permute-start.3) | collective-permute-done | bytes 8224 | tf_op jit(solution)/shard_map/ppermute | solution.py:716
  126.3 0.6 copy-done.10
  126.9 5.5 %air_moved.1 = (f32[2048,128]{1,0:T(8,128)}, f32[2048,128]{1,0:T(8,128)}, f32[512,128]{1,0:T(8,128)}, f32[512,128]{1,0:T(8,128)}) custom-call(s32[2]{0:T(128)S(1)} %pad_add_fusion.place, f32[2048,128]{1,0:T(8,128)} %bitcast.50, f32[2048,128]{1,0:T(8,128)} %bitcast.51, f32[16,128]{1,0:T(8,128)} %copy-done.10, f32[16,128]{1,0:T(8,128)} %copy-done.9), custom_call_target="tpu_custom_call" | custom-call | tf_op jit(solution)/shard_map/air_moved/pallas_call | solution.py:644
  132.4 5.1 %collective-permute-start.5 = (f32[512,128]{1,0:T(8,128)}, f32[512,128]{1,0:T(8,128)}, u32[]{:S(2)}, u32[]{:S(2)}) collective-permute-start(f32[512,128]{1,0:T(8,128)} %get-tuple-element.56), channel_id=1, source_target_pairs={{0,1},{1,2},{2,3},{3,4},{4,5},{5,6},{6,7},{8,9},{9,10},{10,11},{11... | collective-permute-start | bytes 786440 | tf_op jit(solution)/shard_map/ppermute | solution.py:738
  137.5 3.1 %collective-permute-start.6 = (f32[512,128]{1,0:T(8,128)}, f32[512,128]{1,0:T(8,128)}, u32[]{:S(2)}, u32[]{:S(2)}) collective-permute-start(f32[512,128]{1,0:T(8,128)} %get-tuple-element.57), channel_id=1, source_target_pairs={{1,0},{2,1},{3,2},{4,3},{5,4},{6,5},{7,6},{9,8},{10,9},{11,10},{12... | collective-permute-start | bytes 786440 | tf_op jit(solution)/shard_map/ppermute | solution.py:739
  140.7 0.0 copy-start.1
  140.7 1.4 shard_map.151
  142.1 7.2 %all-to-all-start.7 = ((f32[8,64,128]{2,1,0:T(8,128)}), f32[8,64,128]{2,1,0:T(8,128)S(1)}, u32[]{:S(2)}, u32[]{:S(2)}) async-start(f32[8,64,128]{2,1,0:T(8,128)} %bitcast.17), calls=%async_computation.7 | async-start | bytes 524288 | tf_op jit(solution)/shard_map/all_to_all | solution.py:683
  149.3 0.8 pad_maximum_fusion.1
  150.1 2.1 %collective-permute-start.2 = (f32[128,128]{1,0:T(8,128)S(1)}, f32[128,128]{1,0:T(8,128)S(1)}, u32[]{:S(2)}, u32[]{:S(2)}) collective-permute-start(f32[128,128]{1,0:T(8,128)S(1)} %pad_maximum_fusion.1), channel_id=1, source_target_pairs={{0,4},{1,5},{2,6},{3,7},{4,0},{5,1},{6,2},{7,3},{8,12},{9,13},{10,... | collective-permute-start | bytes 196616 | tf_op jit(solution)/shard_map/ppermute | solution.py:721
  152.1 3.7 %collective-permute-done.2 = f32[128,128]{1,0:T(8,128)S(1)} collective-permute-done((f32[128,128]{1,0:T(8,128)S(1)}, f32[128,128]{1,0:T(8,128)S(1)}, u32[]{:S(2)}, u32[]{:S(2)}) %collective-permute-start.2) | collective-permute-done | bytes 65568 | tf_op jit(solution)/shard_map/ppermute | solution.py:721
  155.8 0.8 pad_maximum_fusion.before
  156.6 0.7 copy.15
  157.3 0.6 copy-done.4
  158.0 2.9 %air_finish.1 = f32[2048,128]{1,0:T(8,128)} custom-call(s32[2]{0:T(128)S(1)} %copy-done.4, f32[512,128]{1,0:T(8,128)S(1)} %bitcast.41, f32[256,128]{1,0:T(8,128)S(1)} %pad_maximum_fusion.before, f32[2048,128]{1,0:T(8,128)S(1)} %copy-done.1, f32[2048,128]{1,0:T(8,128)S(1)} %copy-done.2, f32[512,128]{1,0:T(8,128)} %collective-permute-done.5.below, ...), custom_call_target="tpu_custom_call" | custom-call | tf_op jit(solution)/shard_map/air_finish/pallas_call | solution.py:664
  (25 shorter events, 0.1 us)
Async XLA Ops:
  3.2 19.7 %all-to-all-start = ((f32[128,2,128]{2,1,0:T(2,128)}), f32[128,2,128]{2,1,0:T(2,128)S(1)}, u32[]{:S(2)}, u32[]{:S(2)}) async-start(f32[128,2,128]{2,1,0:T(2,128)} %bitcast.48), calls=%async_computation | async-start | bytes 262144 | tf_op jit(solution)/shard_map/all_to_all | solution.py:683
  24.6 14.1 %all-to-all-start.1 = ((f32[128,2,128]{2,1,0:T(2,128)}), f32[128,2,128]{2,1,0:T(2,128)S(1)}, u32[]{:S(2)}, u32[]{:S(2)}) async-start(f32[128,2,128]{2,1,0:T(2,128)} %bitcast.3), calls=%async_computation.1 | async-start | bytes 262144 | tf_op jit(solution)/shard_map/all_to_all | solution.py:683
  40.4 15.3 %all-to-all-start.2 = ((f32[128,4,128]{2,1,0:T(4,128)}), f32[128,4,128]{2,1,0:T(4,128)S(1)}, u32[]{:S(2)}, u32[]{:S(2)}) async-start(f32[128,4,128]{2,1,0:T(4,128)} %bitcast.54), calls=%async_computation.2 | async-start | bytes 524288 | tf_op jit(solution)/shard_map/all_to_all | solution.py:683
  77.7 14.1 %all-to-all-start.4 = ((f32[128,2,128]{2,1,0:T(2,128)}), f32[128,2,128]{2,1,0:T(2,128)S(1)}, u32[]{:S(2)}, u32[]{:S(2)}) async-start(f32[128,2,128]{2,1,0:T(2,128)} %bitcast.55), calls=%async_computation.4 | async-start | bytes 262144 | tf_op jit(solution)/shard_map/all_to_all | solution.py:683
  93.6 4.9 %copy-start.5 = (f32[32,128]{1,0:T(8,128)S(1)}, f32[32,128]{1,0:T(8,128)}, u32[]{:S(2)}) copy-start(f32[32,128]{1,0:T(8,128)} %get-tuple-element.53) | copy-start | bytes 49156
  93.6 16.8 %all-to-all-start.5 = ((f32[128,3,2,128]{3,2,1,0:T(2,128)}), f32[128,3,2,128]{3,2,1,0:T(2,128)S(1)}, u32[]{:S(2)}, u32[]{:S(2)}) async-start(f32[128,3,2,128]{3,2,1,0:T(2,128)} %bitcast.47), calls=%async_computation.5 | async-start | bytes 786432 | tf_op jit(solution)/shard_map/all_to_all | solution.py:683
  98.6 22.6 %collective-permute-start = (f32[32,128]{1,0:T(8,128)S(1)}, f32[32,128]{1,0:T(8,128)S(1)}, u32[]{:S(2)}, u32[]{:S(2)}) collective-permute-start(f32[32,128]{1,0:T(8,128)S(1)} %copy-done.5), channel_id=1, source_target_pairs={{0,1},{1,0},{2,3},{3,2},{4,5},{5,4},{6,7},{7,6},{8,9},{9,8},{10,11... | collective-permute-start | bytes 49160 | tf_op jit(solution)/shard_map/ppermute | solution.py:721
  112.0 28.6 %all-to-all-start.6 = ((f32[128,4,128]{2,1,0:T(4,128)}), f32[128,4,128]{2,1,0:T(4,128)S(1)}, u32[]{:S(2)}, u32[]{:S(2)}) async-start(f32[128,4,128]{2,1,0:T(4,128)} %bitcast.15), calls=%async_computation.6 | async-start | bytes 524288 | tf_op jit(solution)/shard_map/all_to_all | solution.py:683
  117.5 5.0 %collective-permute-start.4 = (f32[16,128]{1,0:T(8,128)S(1)}, f32[16,128]{1,0:T(8,128)S(1)}, u32[]{:S(2)}, u32[]{:S(2)}) collective-permute-start(f32[16,128]{1,0:T(8,128)S(1)} %get-tuple-element.58), channel_id=1, source_target_pairs={{8,0},{16,8},{24,16},{32,24},{40,32},{48,40},{56,48},{64,56},{72,6... | collective-permute-start | bytes 24584 | tf_op jit(solution)/shard_map/ppermute | solution.py:717
  121.1 5.2 %collective-permute-start.3 = (f32[16,128]{1,0:T(8,128)S(1)}, f32[16,128]{1,0:T(8,128)S(1)}, u32[]{:S(2)}, u32[]{:S(2)}) collective-permute-start(f32[16,128]{1,0:T(8,128)S(1)} %get-tuple-element.59), channel_id=1, source_target_pairs={{0,8},{8,16},{16,24},{24,32},{32,40},{40,48},{48,56},{56,64},{64,7... | collective-permute-start | bytes 24584 | tf_op jit(solution)/shard_map/ppermute | solution.py:716
  121.1 11.3 %copy-start.7 = (f32[32,128]{1,0:T(8,128)}, f32[32,128]{1,0:T(8,128)S(1)}, u32[]{:S(2)}) copy-start(f32[32,128]{1,0:T(8,128)S(1)} %collective-permute-done) | copy-start | bytes 49156
  121.8 27.5 %collective-permute-start.1 = (f32[64,128]{1,0:T(8,128)}, f32[64,128]{1,0:T(8,128)}, u32[]{:S(2)}, u32[]{:S(2)}) collective-permute-start(f32[64,128]{1,0:T(8,128)} %pad_maximum_fusion.2), channel_id=1, source_target_pairs={{0,2},{1,3},{2,0},{3,1},{4,6},{5,7},{6,4},{7,5},{8,10},{9,11},{10,... | collective-permute-start | bytes 98312 | tf_op jit(solution)/shard_map/ppermute | solution.py:721
  122.3 4.0 %copy-start.3 = (s32[2]{0:T(128)}, s32[2]{0:T(128)S(1)}, u32[]{:S(2)}) copy-start(s32[2]{0:T(128)S(1)} %pad_add_fusion.place) | copy-start | bytes 28
  122.5 3.8 %copy-start.9 = (f32[16,128]{1,0:T(8,128)}, f32[16,128]{1,0:T(8,128)S(1)}, u32[]{:S(2)}) copy-start(f32[16,128]{1,0:T(8,128)S(1)} %collective-permute-done.4.after) | copy-start | bytes 24580
  126.3 0.6 copy-start.10
  126.9 13.8 %copy-start = (bf16[2,512,512]{2,1,0:T(8,128)(2,1)S(1)}, bf16[2,512,512]{2,1,0:T(8,128)(2,1)}, u32[]{:S(2)}) copy-start(bf16[2,512,512]{2,1,0:T(8,128)(2,1)} %constant.39.clone.refs_3_) | copy-start | bytes 3145732
  132.4 24.9 %collective-permute-start.5 = (f32[512,128]{1,0:T(8,128)}, f32[512,128]{1,0:T(8,128)}, u32[]{:S(2)}, u32[]{:S(2)}) collective-permute-start(f32[512,128]{1,0:T(8,128)} %get-tuple-element.56), channel_id=1, source_target_pairs={{0,1},{1,2},{2,3},{3,4},{4,5},{5,6},{6,7},{8,9},{9,10},{10,11},{11... | collective-permute-start | bytes 786440 | tf_op jit(solution)/shard_map/ppermute | solution.py:738
  137.5 19.7 %collective-permute-start.6 = (f32[512,128]{1,0:T(8,128)}, f32[512,128]{1,0:T(8,128)}, u32[]{:S(2)}, u32[]{:S(2)}) collective-permute-start(f32[512,128]{1,0:T(8,128)} %get-tuple-element.57), channel_id=1, source_target_pairs={{1,0},{2,1},{3,2},{4,3},{5,4},{6,5},{7,6},{9,8},{10,9},{11,10},{12... | collective-permute-start | bytes 786440 | tf_op jit(solution)/shard_map/ppermute | solution.py:739
  140.7 16.6 %copy-start.1 = (f32[2048,128]{1,0:T(8,128)S(1)}, f32[2048,128]{1,0:T(8,128)}, u32[]{:S(2)}) copy-start(f32[2048,128]{1,0:T(8,128)} %get-tuple-element.54.moved) | copy-start | bytes 3145732
  140.7 16.6 %copy-start.2 = (f32[2048,128]{1,0:T(8,128)S(1)}, f32[2048,128]{1,0:T(8,128)}, u32[]{:S(2)}) copy-start(f32[2048,128]{1,0:T(8,128)} %get-tuple-element.55.drift) | copy-start | bytes 3145732
  142.1 7.2 %copy-start.6 = (f32[32,128]{1,0:T(8,128)S(1)}, f32[32,128]{1,0:T(8,128)}, u32[]{:S(2)}) copy-start(f32[32,128]{1,0:T(8,128)} %get-tuple-element.53) | copy-start | bytes 49156
  142.1 15.2 %all-to-all-start.7 = ((f32[8,64,128]{2,1,0:T(8,128)}), f32[8,64,128]{2,1,0:T(8,128)S(1)}, u32[]{:S(2)}, u32[]{:S(2)}) async-start(f32[8,64,128]{2,1,0:T(8,128)} %bitcast.17), calls=%async_computation.7 | async-start | bytes 524288 | tf_op jit(solution)/shard_map/all_to_all | solution.py:683
  149.3 6.6 %copy-start.8 = (f32[32,128]{1,0:T(8,128)S(1)}, f32[32,128]{1,0:T(8,128)}, u32[]{:S(2)}) copy-start(f32[32,128]{1,0:T(8,128)} %copy-done.7) | copy-start | bytes 49156
  150.1 5.8 %collective-permute-start.2 = (f32[128,128]{1,0:T(8,128)S(1)}, f32[128,128]{1,0:T(8,128)S(1)}, u32[]{:S(2)}, u32[]{:S(2)}) collective-permute-start(f32[128,128]{1,0:T(8,128)S(1)} %pad_maximum_fusion.1), channel_id=1, source_target_pairs={{0,4},{1,5},{2,6},{3,7},{4,0},{5,1},{6,2},{7,3},{8,12},{9,13},{10,... | collective-permute-start | bytes 196616 | tf_op jit(solution)/shard_map/ppermute | solution.py:721
  157.3 0.7 copy-start.4
